TPU v7x, 256 devices: a whole 4x4x8 slice. The times are simulated.
256 devices in a mesh: dp: 8 (over x, core), graph: 32 (over z, y).
Axes of the slice: x: 4, y: 4, z: 8, core: 2. Of those that a mesh axis runs over, the one named last changes fastest.
Arguments:
- feats: bfloat16 [8, 16384, 512], P('dp', 'graph'), may hold values from -6 to 6
- grad_out: bfloat16 [8, 16384, 512], P('dp', 'graph'), may hold values from -6 to 6
- w_self: bfloat16 [512, 512], replicated, may hold values from -0.25 to 0.25
- w_neigh: bfloat16 [512, 512], replicated, may hold values from -0.25 to 0.25
- nbr: int32 [8, 16384, 10], P('dp', 'graph'), may hold values from 0 to 2047, as said below
- deg: int32 [8, 16384], P('dp', 'graph'), may hold values from 1 to 10
- hub_rows: int32 [8, 512], P('dp', 'graph'), may hold values from 0 to 511, as said below
- send_rows: int32 [8, 32, 32, 32], P('dp', 'graph'), may hold values from 0 to 511
Outputs:
- out: bfloat16 [8, 16384, 512], P('dp', 'graph')
- grad_feats: bfloat16 [8, 16384, 512], P('dp', 'graph')
- grad_w_self: float32 [512, 512], P('graph')
- grad_w_neigh: float32 [512, 512], P('graph')
Inputs may be any that keep to these rules, and one draw needn't show every extreme that they name: `hub_rows`: within each partition's block of 16 entries the rows are distinct rows of that partition. `nbr`: entries name rows of the partition's table: below 512 its own rows, then 512 hub rows, then 1024 received rows. Only slots below deg are live.
All inputs are finite; a program needn't handle non-finite values.
Results may differ from a plain program's by a relative error of at most 0.007.
Values may be sent and summed in bfloat16 or wider, within the bound.
A program may use at most 64 MiB of HBM per device.

v0:
```python
import jax
import jax.numpy as jnp
from jax import lax
from jax.sharding import PartitionSpec as P


def shards(feats, grad_out, w_self, w_neigh, nbr, deg, hub_rows, send_rows):
    own = feats[0]
    grads = grad_out[0]
    rows, width = own.shape
    idx = nbr[0]
    dcount = deg[0]
    hub_idx = hub_rows[0]
    sent_idx = send_rows[0, 0]
    hub_local = own[hub_idx]
    hubs = lax.all_gather(hub_local, "graph", axis=0, tiled=True)
    outgoing = own[sent_idx]
    incoming = lax.all_to_all(outgoing, "graph", split_axis=0, concat_axis=0, tiled=True)
    nhub = hubs.shape[0]
    table = jnp.concatenate([own, hubs, incoming.reshape(-1, width)], axis=0)
    slots = idx.shape[1]
    live = jnp.arange(slots)[None, :] < dcount[:, None]
    total = jnp.zeros((rows, width), jnp.float32)
    for k in range(slots):
        total = total + jnp.where(live[:, k : k + 1], table[idx[:, k]].astype(jnp.float32), 0.0)
    degree = dcount.astype(jnp.float32)[:, None]
    agg = (total / degree).astype(jnp.bfloat16)
    result = (
        jnp.dot(own, w_self, preferred_element_type=jnp.float32)
        + jnp.dot(agg, w_neigh, preferred_element_type=jnp.float32)
    ).astype(jnp.bfloat16)
    trans = (((1,), (1,)), ((), ()))
    back = lax.dot_general(grads, w_neigh, trans, preferred_element_type=jnp.float32) / degree
    height = table.shape[0]
    dtable = jnp.zeros((height, width), jnp.float32)
    for k in range(slots):
        target = jnp.where(live[:, k], idx[:, k], height)
        dtable = dtable.at[target].add(back, mode="drop")
    hub_back = lax.psum_scatter(
        dtable[rows : rows + nhub].astype(jnp.bfloat16), "graph", scatter_dimension=0, tiled=True
    ).astype(jnp.float32)
    recv_back = lax.all_to_all(
        dtable[rows + nhub :].reshape(incoming.shape).astype(jnp.bfloat16),
        "graph",
        split_axis=0,
        concat_axis=0,
        tiled=True,
    ).astype(jnp.float32)
    inner = (((0,), (0,)), ((), ()))
    dws = lax.dot_general(own, grads, inner, preferred_element_type=jnp.float32)
    dwn = lax.dot_general(agg, grads, inner, preferred_element_type=jnp.float32)
    dlocal = (
        lax.dot_general(grads, w_self, trans, preferred_element_type=jnp.float32) + dtable[:rows]
    )
    dlocal = dlocal.at[hub_idx].add(hub_back)
    dlocal = dlocal.at[sent_idx.reshape(-1)].add(recv_back.reshape(-1, width))
    grad_rows = dlocal.astype(jnp.bfloat16)
    share = width // lax.axis_size("graph")
    sum_self, sum_neigh = lax.psum((dws, dwn), ("dp", "graph"))
    start = lax.axis_index("graph") * share
    sum_self = lax.dynamic_slice_in_dim(sum_self, start, share, 0)
    sum_neigh = lax.dynamic_slice_in_dim(sum_neigh, start, share, 0)
    count = lax.axis_size("dp") * lax.axis_size("graph") * rows
    scale = 1.0 / jnp.sqrt(jnp.float32(count))
    return (result[None], grad_rows[None], sum_self * scale, sum_neigh * scale)


def solution(mesh):
    placed = (
        P("dp", "graph", None),
        P("dp", "graph", None),
        P(),
        P(),
        P("dp", "graph", None),
        P("dp", "graph"),
        P("dp", "graph"),
        P("dp", "graph", None, None),
    )
    return jax.shard_map(
        shards,
        mesh=mesh,
        in_specs=placed,
        out_specs=(
            P("dp", "graph", None),
            P("dp", "graph", None),
            P("graph", None),
            P("graph", None),
        ),
        check_vma=False,
    )
```

profile of v0, /device:TPU:2, one launch (start us, length us, event | category | flops | bytes accessed | tf_op | source)
XLA Modules:
  0.0 481.6 jit_solution(7234979474906921619)
XLA Ops:
  8.0 0.8 compare_select_fusion
  8.8 0.1 reshape.124
  8.9 6.3 %gather_fusion.1 = bf16[1024,512]{1,0:T(8,128)(2,1)} fusion(bf16[512,512]{1,0:T(8,128)(2,1)} %bitcast.64, s32[1024]{0:T(1024)S(1)} %broadcast_clamp_fusion), kind=kCustom, calls=%fused_computation.1 | custom fusion | bytes 2101248 | tf_op jit(solution)/shard_map/gather | solution.py:17
  15.2 11.6 %all-to-all-start = ((bf16[32,32,512]{2,1,0:T(8,128)(2,1)}), bf16[32,32,512]{2,1,0:T(8,128)(2,1)}, u32[]{:S(2)}, u32[]{:S(2)}) async-start(bf16[32,32,512]{2,1,0:T(8,128)(2,1)} %bitcast.5), calls=%async_computation | async-start | bytes 2097152 | tf_op jit(solution)/shard_map/all_to_all | solution.py:18
  26.8 0.0 reduce-scatter.2.cloned.1.call-start
  27.0 0.5 convolution_divide_fusion
  27.5 5.7 %scatter_custom_fusion = f32[2048,512]{1,0:T(8,128)} fusion(s32[512]{0:T(512)S(1)} %bitcast.92, f32[512,512]{1,0:T(8,128)S(1)} %convolution_divide_fusion, f32[]{:T(128)} %constant.10.clone.1), kind=kCustom, calls=%fused_computation.27 | custom fusion | flops 262144 | bytes 4194308 | tf_op jit(solution)/shard_map/scatter-add | solution.py:38
  33.2 7.6 %scatter_fusion = f32[2048,512]{1,0:T(8,128)} fusion(f32[2048,512]{1,0:T(8,128)} %scatter_custom_fusion, s32[512]{0:T(512)S(1)} %bitcast.77, f32[512,512]{1,0:T(8,128)S(1)} %convolution_divide_fusion), kind=kCustom, calls=%fused_computation.13 | custom fusion | flops 262144 | bytes 3147776 | tf_op jit(solution)/shard_map/scatter-add | solution.py:38
  40.8 8.1 %scatter_fusion.1 = f32[2048,512]{1,0:T(8,128)} fusion(f32[2048,512]{1,0:T(8,128)} %scatter_fusion, s32[512]{0:T(512)S(1)} %bitcast.76, f32[512,512]{1,0:T(8,128)S(1)} %convolution_divide_fusion), kind=kCustom, calls=%fused_computation.14 | custom fusion | flops 262144 | bytes 3147776 | tf_op jit(solution)/shard_map/scatter-add | solution.py:38
  49.0 7.6 %scatter_fusion.2 = f32[2048,512]{1,0:T(8,128)} fusion(f32[2048,512]{1,0:T(8,128)} %scatter_fusion.1, s32[512]{0:T(512)S(1)} %bitcast.75, f32[512,512]{1,0:T(8,128)S(1)} %convolution_divide_fusion), kind=kCustom, calls=%fused_computation.15 | custom fusion | flops 262144 | bytes 3147776 | tf_op jit(solution)/shard_map/scatter-add | solution.py:38
  56.6 7.6 %scatter_fusion.3 = f32[2048,512]{1,0:T(8,128)} fusion(f32[2048,512]{1,0:T(8,128)} %scatter_fusion.2, s32[512]{0:T(512)S(1)} %bitcast.74, f32[512,512]{1,0:T(8,128)S(1)} %convolution_divide_fusion), kind=kCustom, calls=%fused_computation.16 | custom fusion | flops 262144 | bytes 3147776 | tf_op jit(solution)/shard_map/scatter-add | solution.py:38
  64.3 7.6 %scatter_fusion.4 = f32[2048,512]{1,0:T(8,128)} fusion(f32[2048,512]{1,0:T(8,128)} %scatter_fusion.3, s32[512]{0:T(512)S(1)} %bitcast.73, f32[512,512]{1,0:T(8,128)S(1)} %convolution_divide_fusion), kind=kCustom, calls=%fused_computation.17 | custom fusion | flops 262144 | bytes 3147776 | tf_op jit(solution)/shard_map/scatter-add | solution.py:38
  71.9 7.8 %scatter_fusion.5 = f32[2048,512]{1,0:T(8,128)} fusion(f32[2048,512]{1,0:T(8,128)} %scatter_fusion.4, s32[512]{0:T(512)S(1)} %bitcast.72, f32[512,512]{1,0:T(8,128)S(1)} %convolution_divide_fusion), kind=kCustom, calls=%fused_computation.18 | custom fusion | flops 262144 | bytes 3147776 | tf_op jit(solution)/shard_map/scatter-add | solution.py:38
  79.7 7.6 %scatter_fusion.6 = f32[2048,512]{1,0:T(8,128)} fusion(f32[2048,512]{1,0:T(8,128)} %scatter_fusion.5, s32[512]{0:T(512)S(1)} %bitcast.71, f32[512,512]{1,0:T(8,128)S(1)} %convolution_divide_fusion), kind=kCustom, calls=%fused_computation.19 | custom fusion | flops 262144 | bytes 3147776 | tf_op jit(solution)/shard_map/scatter-add | solution.py:38
  87.4 7.6 %scatter_fusion.7 = f32[2048,512]{1,0:T(8,128)} fusion(f32[2048,512]{1,0:T(8,128)} %scatter_fusion.6, s32[512]{0:T(512)S(1)} %bitcast.78, f32[512,512]{1,0:T(8,128)S(1)} %convolution_divide_fusion), kind=kCustom, calls=%fused_computation.20 | custom fusion | flops 262144 | bytes 3147776 | tf_op jit(solution)/shard_map/scatter-add | solution.py:38
  95.0 7.6 %scatter_fusion.8 = f32[2048,512]{1,0:T(8,128)} fusion(f32[2048,512]{1,0:T(8,128)} %scatter_fusion.7, s32[512]{0:T(512)S(1)} %bitcast.70, f32[512,512]{1,0:T(8,128)S(1)} %convolution_divide_fusion), kind=kCustom, calls=%fused_computation.21 | custom fusion | flops 262144 | bytes 3147776 | tf_op jit(solution)/shard_map/scatter-add | solution.py:38
  102.7 2.5 convert.5
  105.2 0.8 slice.159
  106.0 1.0 slice.160
  107.1 0.1 reshape_squeeze.3
  107.2 0.6 gather_fusion
  107.9 0.1 slice_reduce_fusion.9
  108.0 54.8 %all-gather = bf16[512,512]{1,0:T(8,128)(2,1)} all-gather(bf16[16,512]{1,0:T(8,128)(2,1)S(1)} %gather_fusion), channel_id=2, replica_groups=mesh['dp'=8,'graph'=32] {'graph'}, dimensions={0}, use_global_device_ids=true | all-gather | bytes 540672 | tf_op jit(solution)/shard_map/all_gather | solution.py:16
  162.8 8.5 %all-to-all-start.1 = ((bf16[32,32,512]{2,1,0:T(8,128)(2,1)}), bf16[32,32,512]{2,1,0:T(8,128)(2,1)}, u32[]{:S(2)}, u32[]{:S(2)}) async-start(bf16[32,32,512]{2,1,0:T(8,128)(2,1)} %bitcast.67), calls=%async_computation.2 | async-start | bytes 2097152 | tf_op jit(solution)/shard_map/all_to_all | solution.py:42
  171.3 0.3 all-reduce.3.cloned.1.call-start
  171.5 1.5 fusion.8
  173.0 1.5 pad_maximum_fusion
  174.5 2.6 gather_fusion.10
  177.1 2.6 gather_fusion.11
  179.8 2.6 gather_fusion.2
  182.4 2.6 gather_fusion.3
  185.0 2.6 gather_fusion.4
  187.6 2.6 gather_fusion.5
  190.3 2.6 gather_fusion.6
  192.9 2.6 gather_fusion.7
  195.5 2.6 gather_fusion.8
  198.2 2.6 gather_fusion.9
  200.8 4.1 divide_convert_fusion
  204.9 1.4 fusion.6
  206.4 1.4 fusion.16
  207.8 1.8 convolution_add_fusion
  209.6 116.8 %reduce-scatter.2.cloned.1.call-done = bf16[16,512]{1,0:T(8,128)(2,1)} async-done(((bf16[512,512]{1,0:T(8,128)(2,1)}), bf16[16,512]{1,0:T(8,128)(2,1)}) %reduce-scatter.2.cloned.1.call-update) | async-done | bytes 16400 | tf_op jit(solution)/shard_map/reduce_scatter | solution.py:39
  326.3 1.3 scatter_custom_fusion.10
  327.6 7.9 %scatter_custom_fusion.11 = f32[512,512]{1,0:T(8,128)S(1)} fusion(f32[512,512]{1,0:T(8,128)S(1)} %scatter_custom_fusion.10, s32[1024]{0:T(1024)S(1)} %bitcast.91, bf16[1024,512]{1,0:T(8,128)(2,1)} %bitcast.33), kind=kCustom, calls=%fused_computation.25 | custom fusion | flops 1048576 | bytes 2097152 | tf_op jit(solution)/shard_map/scatter-add | solution.py:56
  335.5 2.5 fusion.5
  338.0 0.9 convert_bitcast_fusion
  338.9 133.6 %all-reduce.3.cloned.1.call-done = (f32[512,512]{1,0:T(8,128)}, f32[512,512]{1,0:T(8,128)}) async-done(((f32[512,512]{1,0:T(8,128)}, f32[512,512]{1,0:T(8,128)}), (f32[512,512]{1,0:T(8,128)}, f32[512,512]{1,0:T(8,128)})) %all-reduce.3.cloned.1.call-update) | async-done | bytes 2097168 | tf_op jit(solution)/shard_map/psum | solution.py:59
  472.4 1.4 dynamic-slice_multiply_fusion
  (41 shorter events, 0.3 us)
Async XLA Ops:
  8.0 19.0 %copy-start = (bf16[1,512,512]{2,1,0:T(8,128)(2,1)S(1)}, bf16[1,512,512]{2,1,0:T(8,128)(2,1)}, u32[]{:S(2)}) copy-start(bf16[1,512,512]{2,1,0:T(8,128)(2,1)} %param.9) | copy-start | bytes 1572868
  8.9 18.0 %copy-start.7 = (s32[1,512]{1,0:T(1,128)S(1)}, s32[1,512]{1,0:T(1,128)}, u32[]{:S(2)}) copy-start(s32[1,512]{1,0:T(1,128)} %param.13) | copy-start | bytes 6148
  8.9 18.0 %copy-start.6 = (s32[1,512,10]{1,0,2:T(1,128)S(1)}, s32[1,512,10]{1,0,2:T(1,128)}, u32[]{:S(2)}) copy-start(s32[1,512,10]{1,0,2:T(1,128)} %param.12) | copy-start | bytes 61444
  8.9 18.1 %copy-start.3 = (bf16[512,512]{1,0:T(8,128)(2,1)S(1)}, bf16[512,512]{1,0:T(8,128)(2,1)}, u32[]{:S(2)}) copy-start(bf16[512,512]{1,0:T(8,128)(2,1)} %param.11) | copy-start | bytes 1572868
  15.2 147.6 %all-to-all-start = ((bf16[32,32,512]{2,1,0:T(8,128)(2,1)}), bf16[32,32,512]{2,1,0:T(8,128)(2,1)}, u32[]{:S(2)}, u32[]{:S(2)}) async-start(bf16[32,32,512]{2,1,0:T(8,128)(2,1)} %bitcast.5), calls=%async_computation | async-start | bytes 2097152 | tf_op jit(solution)/shard_map/all_to_all | solution.py:18
  26.8 299.6 %reduce-scatter.2.cloned.1.call-start = ((), (), s32[]{:S(2)}) async-start(), calls=%async_computation.3 | async-start | bytes 540672 | tf_op jit(solution)/shard_map/reduce_scatter | solution.py:39
  102.6 4.4 copy-start.5
  102.6 4.5 copy-start.8
  102.7 4.5 copy-start.1
  162.8 164.8 %all-to-all-start.1 = ((bf16[32,32,512]{2,1,0:T(8,128)(2,1)}), bf16[32,32,512]{2,1,0:T(8,128)(2,1)}, u32[]{:S(2)}, u32[]{:S(2)}) async-start(bf16[32,32,512]{2,1,0:T(8,128)(2,1)} %bitcast.67), calls=%async_computation.2 | async-start | bytes 2097152 | tf_op jit(solution)/shard_map/all_to_all | solution.py:42
  171.3 301.2 %all-reduce.3.cloned.1.call-start = ((), (), s32[]{:S(2)}) async-start(), calls=%async_computation.4 | async-start | bytes 4194304 | tf_op jit(solution)/shard_map/psum | solution.py:59
  200.8 5.6 %copy-start.2 = (bf16[512,512]{1,0:T(8,128)(2,1)S(1)}, bf16[512,512]{1,0:T(8,128)(2,1)}, u32[]{:S(2)}) copy-start(bf16[512,512]{1,0:T(8,128)(2,1)} %param.10) | copy-start | bytes 1572868
  207.8 127.7 %copy-start.4 = (bf16[512,512]{1,0:T(8,128)(2,1)S(1)}, bf16[512,512]{1,0:T(8,128)(2,1)}, u32[]{:S(2)}) copy-start(bf16[512,512]{1,0:T(8,128)(2,1)} %param.11) | copy-start | bytes 1572868
Sparse Core Ops, SparseCore 0:
  106.1 220.1 reduce-scatter.1
Sparse Core Ops, SparseCore 1:
  206.4 265.9 all-reduce.2
where the time goes:
time: 490 us; the launch traced here: 482 us
  waiting for transfers between devices  250 us (51%)
  other arithmetic  95.6 us (20%)
  blocking collectives  54.8 us (11%)
  local copies, waits for them, and re-layouts  35.2 us (7%)
  starting transfers between devices  20.4 us (4%)
  between operations  16.1 us (3%)
  matrix products  9.02 us (2%)
    psum x1, waiting for transfers between devices, shards(): sum_self, sum_neigh = lax.psum((dws, dwn), ('dp', 'graph'))  134 us
    reduce_scatter x1, waiting for transfers between devices, shards(): lax.psum_scatter(dtable[rows:rows + nhub].astype(jnp.bfloat16), 'graph',...  117 us
    scatter-add x10, other arithmetic, shards(): dtable = dtable.at[target].add(back, mode='drop')  75.1 us
    all_gather x1, blocking collectives, shards(): hubs = lax.all_gather(hub_local, 'graph', axis=0, tiled=True)  54.8 us
    gather x10, local copies, waits for them, and re-layouts, shards(): table[idx[:, k]].astype(jnp.float32)  26.2 us
    all_to_all x1, starting transfers between devices, shards(): lax.all_to_all(outgoing, 'graph', split_axis=0, concat_axis=0, tiled=True)  11.6 us
  transfers between devices with their start and end apart: 4, of which 2 were waited for; matrix products, arithmetic and copies ran while one was open for 27% of the time, Pallas kernels for 0%

commit v1 on v0

--- a/solution.py
+++ b/solution.py
@@ -13,7 +13,9 @@
     hub_idx = hub_rows[0]
     sent_idx = send_rows[0, 0]
     hub_local = own[hub_idx]
-    hubs = lax.all_gather(hub_local, "graph", axis=0, tiled=True)
+    hubs = jnp.concatenate(
+        lax.all_to_all(jnp.stack([hub_local] * lax.axis_size("graph")), "graph", 0, 0), axis=0
+    )
     outgoing = own[sent_idx]
     incoming = lax.all_to_all(outgoing, "graph", split_axis=0, concat_axis=0, tiled=True)
     nhub = hubs.shape[0]

time: 490 us -> 457 us (0.933)
  blocking collectives: 54.8 us -> 0 us
  waiting for transfers between devices: 250 us -> 262 us
  starting transfers between devices: 20.4 us -> 26.4 us
    all_gather x1 -> x0, blocking collectives: 54.8 us -> none  [shards(): hubs = lax.all_gather(hub_local, 'graph', axis=0, tiled=True)]
    reduce_scatter x1, waiting for transfers between devices: 117 us -> 170 us  [shards(): lax.psum_scatter(dtable[rows:rows + nhub].astype(jnp.bfloat16), 'graph',...]
    psum x1, waiting for transfers between devices: 134 us -> 82.1 us  [shards(): sum_self, sum_neigh = lax.psum((dws, dwn), ('dp', 'graph'))]
    all_to_all x0 -> x1, starting transfers between devices: none -> 11.5 us  [shards(): lax.all_to_all(jnp.stack([hub_local] * lax.axis_size('graph')), 'graph',...]
    all_to_all x0 -> x1, waiting for transfers between devices: none -> 10.4 us  [shards(): lax.all_to_all(jnp.stack([hub_local] * lax.axis_size('graph')), 'graph',...]
    all_to_all x1, starting transfers between devices: 11.6 us -> 4.77 us  [shards(): lax.all_to_all(outgoing, 'graph', split_axis=0, concat_axis=0, tiled=True)]
  transfers between devices with their start and end apart: 4 -> 5, of which waited for: 2 -> 3; matrix products, arithmetic and copies ran while one was open for 27% -> 31% of each run, Pallas kernels for 0% -> 0%
where the time goes in v1:
time: 457 us; the launch traced here: 448 us
  waiting for transfers between devices  262 us (57%)
  other arithmetic  97 us (21%)
  local copies, waits for them, and re-layouts  36.7 us (8%)
  starting transfers between devices  26.4 us (6%)
  between operations  16 us (4%)
  matrix products  9.02 us (2%)
    reduce_scatter x1, waiting for transfers between devices, shards(): lax.psum_scatter(dtable[rows:rows + nhub].astype(jnp.bfloat16), 'graph',...  170 us
    psum x1, waiting for transfers between devices, shards(): sum_self, sum_neigh = lax.psum((dws, dwn), ('dp', 'graph'))  82.1 us
    scatter-add x10, other arithmetic, shards(): dtable = dtable.at[target].add(back, mode='drop')  75.1 us
    gather x10, local copies, waits for them, and re-layouts, shards(): table[idx[:, k]].astype(jnp.float32)  26.2 us
    all_to_all x1, starting transfers between devices, shards(): lax.all_to_all(jnp.stack([hub_local] * lax.axis_size('graph')), 'graph',...  11.5 us
    all_to_all x1, waiting for transfers between devices, shards(): lax.all_to_all(jnp.stack([hub_local] * lax.axis_size('graph')), 'graph',...  10.4 us
    all_to_all x1, starting transfers between devices, shards(): lax.all_to_all(dtable[rows + nhub:].reshape(incoming.shape).astype(jnp.bf...  9.84 us
  transfers between devices with their start and end apart: 5, of which 3 were waited for; matrix products, arithmetic and copies ran while one was open for 31% of the time, Pallas kernels for 0%

profile of v1, /device:TPU:2, one launch (start us, length us, event | category | flops | bytes accessed | tf_op | source)
XLA Modules:
  0.0 447.6 jit_solution(8109289335680114093)
XLA Ops:
  8.0 0.7 fusion.14
  8.8 1.7 gather_fusion
  10.5 0.9 stack.2
  11.3 11.5 %all-to-all-start = ((bf16[32,16,512]{2,1,0:T(8,128)(2,1)}), bf16[32,16,512]{2,1,0:T(8,128)(2,1)S(1)}, u32[]{:S(2)}, u32[]{:S(2)}) async-start(bf16[32,16,512]{2,1,0:T(8,128)(2,1)} %stack.2), calls=%async_computation | async-start | bytes 1048576 | tf_op jit(solution)/shard_map/all_to_all | solution.py:17
  22.8 0.7 copy.14
  23.6 0.7 convert_element_type.65
  24.2 0.7 compare_select_fusion
  25.1 5.1 %gather_fusion.1 = bf16[1024,512]{1,0:T(8,128)(2,1)} fusion(bf16[512,512]{1,0:T(8,128)(2,1)S(1)} %bitcast.66, s32[1024]{0:T(1024)S(1)} %broadcast_clamp_fusion), kind=kCustom, calls=%fused_computation.1 | custom fusion | bytes 2101248 | tf_op jit(solution)/shard_map/gather | solution.py:19
  30.1 10.4 %all-to-all-done = bf16[32,16,512]{2,1,0:T(8,128)(2,1)S(1)} async-done(((bf16[32,16,512]{2,1,0:T(8,128)(2,1)}), bf16[32,16,512]{2,1,0:T(8,128)(2,1)S(1)}, u32[]{:S(2)}, u32[]{:S(2)}) %all-to-all-start) | async-done | bytes 524320 | tf_op jit(solution)/shard_map/all_to_all | solution.py:17
  40.6 4.8 %all-to-all-start.1 = ((bf16[32,32,512]{2,1,0:T(8,128)(2,1)}), bf16[32,32,512]{2,1,0:T(8,128)(2,1)}, u32[]{:S(2)}, u32[]{:S(2)}) async-start(bf16[32,32,512]{2,1,0:T(8,128)(2,1)} %bitcast.6), calls=%async_computation.1 | async-start | bytes 2097152 | tf_op jit(solution)/shard_map/all_to_all | solution.py:20
  45.5 0.5 convolution_divide_fusion
  46.0 5.7 %scatter_custom_fusion = f32[2048,512]{1,0:T(8,128)} fusion(s32[512]{0:T(512)S(1)} %bitcast.94, f32[512,512]{1,0:T(8,128)S(1)} %convolution_divide_fusion, f32[]{:T(128)} %constant.10.clone.1), kind=kCustom, calls=%fused_computation.27 | custom fusion | flops 262144 | bytes 4194308 | tf_op jit(solution)/shard_map/scatter-add | solution.py:40
  51.7 7.6 %scatter_fusion = f32[2048,512]{1,0:T(8,128)} fusion(f32[2048,512]{1,0:T(8,128)} %scatter_custom_fusion, s32[512]{0:T(512)S(1)} %bitcast.79, f32[512,512]{1,0:T(8,128)S(1)} %convolution_divide_fusion), kind=kCustom, calls=%fused_computation.13 | custom fusion | flops 262144 | bytes 3147776 | tf_op jit(solution)/shard_map/scatter-add | solution.py:40
  59.3 8.1 %scatter_fusion.1 = f32[2048,512]{1,0:T(8,128)} fusion(f32[2048,512]{1,0:T(8,128)} %scatter_fusion, s32[512]{0:T(512)S(1)} %bitcast.78, f32[512,512]{1,0:T(8,128)S(1)} %convolution_divide_fusion), kind=kCustom, calls=%fused_computation.14 | custom fusion | flops 262144 | bytes 3147776 | tf_op jit(solution)/shard_map/scatter-add | solution.py:40
  67.5 7.6 %scatter_fusion.2 = f32[2048,512]{1,0:T(8,128)} fusion(f32[2048,512]{1,0:T(8,128)} %scatter_fusion.1, s32[512]{0:T(512)S(1)} %bitcast.77, f32[512,512]{1,0:T(8,128)S(1)} %convolution_divide_fusion), kind=kCustom, calls=%fused_computation.15 | custom fusion | flops 262144 | bytes 3147776 | tf_op jit(solution)/shard_map/scatter-add | solution.py:40
  75.1 7.6 %scatter_fusion.3 = f32[2048,512]{1,0:T(8,128)} fusion(f32[2048,512]{1,0:T(8,128)} %scatter_fusion.2, s32[512]{0:T(512)S(1)} %bitcast.76, f32[512,512]{1,0:T(8,128)S(1)} %convolution_divide_fusion), kind=kCustom, calls=%fused_computation.16 | custom fusion | flops 262144 | bytes 3147776 | tf_op jit(solution)/shard_map/scatter-add | solution.py:40
  82.8 7.6 %scatter_fusion.4 = f32[2048,512]{1,0:T(8,128)} fusion(f32[2048,512]{1,0:T(8,128)} %scatter_fusion.3, s32[512]{0:T(512)S(1)} %bitcast.75, f32[512,512]{1,0:T(8,128)S(1)} %convolution_divide_fusion), kind=kCustom, calls=%fused_computation.17 | custom fusion | flops 262144 | bytes 3147776 | tf_op jit(solution)/shard_map/scatter-add | solution.py:40
  90.4 7.8 %scatter_fusion.5 = f32[2048,512]{1,0:T(8,128)} fusion(f32[2048,512]{1,0:T(8,128)} %scatter_fusion.4, s32[512]{0:T(512)S(1)} %bitcast.74, f32[512,512]{1,0:T(8,128)S(1)} %convolution_divide_fusion), kind=kCustom, calls=%fused_computation.18 | custom fusion | flops 262144 | bytes 3147776 | tf_op jit(solution)/shard_map/scatter-add | solution.py:40
  98.2 7.6 %scatter_fusion.6 = f32[2048,512]{1,0:T(8,128)} fusion(f32[2048,512]{1,0:T(8,128)} %scatter_fusion.5, s32[512]{0:T(512)S(1)} %bitcast.73, f32[512,512]{1,0:T(8,128)S(1)} %convolution_divide_fusion), kind=kCustom, calls=%fused_computation.19 | custom fusion | flops 262144 | bytes 3147776 | tf_op jit(solution)/shard_map/scatter-add | solution.py:40
  105.9 7.6 %scatter_fusion.7 = f32[2048,512]{1,0:T(8,128)} fusion(f32[2048,512]{1,0:T(8,128)} %scatter_fusion.6, s32[512]{0:T(512)S(1)} %bitcast.80, f32[512,512]{1,0:T(8,128)S(1)} %convolution_divide_fusion), kind=kCustom, calls=%fused_computation.20 | custom fusion | flops 262144 | bytes 3147776 | tf_op jit(solution)/shard_map/scatter-add | solution.py:40
  113.5 7.6 %scatter_fusion.8 = f32[2048,512]{1,0:T(8,128)} fusion(f32[2048,512]{1,0:T(8,128)} %scatter_fusion.7, s32[512]{0:T(512)S(1)} %bitcast.72, f32[512,512]{1,0:T(8,128)S(1)} %convolution_divide_fusion), kind=kCustom, calls=%fused_computation.21 | custom fusion | flops 262144 | bytes 3147776 | tf_op jit(solution)/shard_map/scatter-add | solution.py:40
  121.2 2.5 convert.5
  123.6 0.8 slice.159
  124.5 1.0 slice.160
  125.8 9.8 %all-to-all-start.2 = ((bf16[32,32,512]{2,1,0:T(8,128)(2,1)}), bf16[32,32,512]{2,1,0:T(8,128)(2,1)}, u32[]{:S(2)}, u32[]{:S(2)}) async-start(bf16[32,32,512]{2,1,0:T(8,128)(2,1)} %bitcast.68), calls=%async_computation.3 | async-start | bytes 2097152 | tf_op jit(solution)/shard_map/all_to_all | solution.py:44
  136.0 1.5 fusion.8
  137.4 1.5 pad_maximum_fusion
  138.9 2.6 gather_fusion.10
  141.6 2.6 gather_fusion.11
  144.2 2.6 gather_fusion.2
  146.8 2.6 gather_fusion.3
  149.4 2.6 gather_fusion.4
  152.1 2.6 gather_fusion.5
  154.7 2.6 gather_fusion.6
  157.3 2.6 gather_fusion.7
  160.0 2.6 gather_fusion.8
  162.6 2.6 gather_fusion.9
  165.2 4.1 divide_convert_fusion
  169.3 1.4 fusion.6
  170.8 1.4 fusion.16
  172.2 1.8 convolution_add_fusion
  174.0 169.8 %reduce-scatter.2.cloned.1.call-done = bf16[16,512]{1,0:T(8,128)(2,1)} async-done(((bf16[512,512]{1,0:T(8,128)(2,1)}), bf16[16,512]{1,0:T(8,128)(2,1)}) %reduce-scatter.2.cloned.1.call-update) | async-done | bytes 16400 | tf_op jit(solution)/shard_map/reduce_scatter | solution.py:41
  343.8 1.3 scatter_custom_fusion.10
  345.1 7.9 %scatter_custom_fusion.11 = f32[512,512]{1,0:T(8,128)S(1)} fusion(f32[512,512]{1,0:T(8,128)S(1)} %scatter_custom_fusion.10, s32[1024]{0:T(1024)S(1)} %bitcast.93, bf16[1024,512]{1,0:T(8,128)(2,1)} %bitcast.34), kind=kCustom, calls=%fused_computation.25 | custom fusion | flops 1048576 | bytes 2097152 | tf_op jit(solution)/shard_map/scatter-add | solution.py:58
  353.0 2.5 fusion.5
  355.5 0.9 convert_bitcast_fusion
  356.3 82.1 %all-reduce.3.cloned.1.call-done = (f32[512,512]{1,0:T(8,128)}, f32[512,512]{1,0:T(8,128)}) async-done(((f32[512,512]{1,0:T(8,128)}, f32[512,512]{1,0:T(8,128)}), (f32[512,512]{1,0:T(8,128)}, f32[512,512]{1,0:T(8,128)})) %all-reduce.3.cloned.1.call-update) | async-done | bytes 2097168 | tf_op jit(solution)/shard_map/psum | solution.py:61
  438.5 1.4 dynamic-slice_multiply_fusion
  (41 shorter events, 0.8 us)
Async XLA Ops:
  8.0 37.5 %copy-start = (bf16[1,512,512]{2,1,0:T(8,128)(2,1)S(1)}, bf16[1,512,512]{2,1,0:T(8,128)(2,1)}, u32[]{:S(2)}) copy-start(bf16[1,512,512]{2,1,0:T(8,128)(2,1)} %param.9) | copy-start | bytes 1572868
  8.0 17.0 %copy-start.1 = (bf16[1,512,512]{2,1,0:T(8,128)(2,1)S(1)}, bf16[1,512,512]{2,1,0:T(8,128)(2,1)}, u32[]{:S(2)}) copy-start(bf16[1,512,512]{2,1,0:T(8,128)(2,1)} %param.8) | copy-start | bytes 1572868
  11.3 29.3 %all-to-all-start = ((bf16[32,16,512]{2,1,0:T(8,128)(2,1)}), bf16[32,16,512]{2,1,0:T(8,128)(2,1)S(1)}, u32[]{:S(2)}, u32[]{:S(2)}) async-start(bf16[32,16,512]{2,1,0:T(8,128)(2,1)} %stack.2), calls=%async_computation | async-start | bytes 1048576 | tf_op jit(solution)/shard_map/all_to_all | solution.py:17
  25.0 5.1 %copy-start.7 = (s32[1,512]{1,0:T(1,128)S(1)}, s32[1,512]{1,0:T(1,128)}, u32[]{:S(2)}) copy-start(s32[1,512]{1,0:T(1,128)} %param.13) | copy-start | bytes 6148
  25.1 20.4 %copy-start.4 = (bf16[512,512]{1,0:T(8,128)(2,1)S(1)}, bf16[512,512]{1,0:T(8,128)(2,1)}, u32[]{:S(2)}) copy-start(bf16[512,512]{1,0:T(8,128)(2,1)} %param.11) | copy-start | bytes 1572868
  40.6 4.8 %copy-start.3 = (bf16[32,16,512]{2,1,0:T(8,128)(2,1)}, bf16[32,16,512]{2,1,0:T(8,128)(2,1)S(1)}, u32[]{:S(2)}) copy-start(bf16[32,16,512]{2,1,0:T(8,128)(2,1)S(1)} %all-to-all-done) | copy-start | bytes 1572868
  40.6 85.2 %all-to-all-start.1 = ((bf16[32,32,512]{2,1,0:T(8,128)(2,1)}), bf16[32,32,512]{2,1,0:T(8,128)(2,1)}, u32[]{:S(2)}, u32[]{:S(2)}) async-start(bf16[32,32,512]{2,1,0:T(8,128)(2,1)} %bitcast.6), calls=%async_computation.1 | async-start | bytes 2097152 | tf_op jit(solution)/shard_map/all_to_all | solution.py:20
  45.4 298.5 %reduce-scatter.2.cloned.1.call-start = ((), (), s32[]{:S(2)}) async-start(), calls=%async_computation.4 | async-start | bytes 540672 | tf_op jit(solution)/shard_map/reduce_scatter | solution.py:41
  121.2 4.4 copy-start.6
  125.8 219.3 %all-to-all-start.2 = ((bf16[32,32,512]{2,1,0:T(8,128)(2,1)}), bf16[32,32,512]{2,1,0:T(8,128)(2,1)}, u32[]{:S(2)}, u32[]{:S(2)}) async-start(bf16[32,32,512]{2,1,0:T(8,128)(2,1)} %bitcast.68), calls=%async_computation.3 | async-start | bytes 2097152 | tf_op jit(solution)/shard_map/all_to_all | solution.py:44
  135.7 302.8 %all-reduce.3.cloned.1.call-start = ((), (), s32[]{:S(2)}) async-start(), calls=%async_computation.5 | async-start | bytes 4194304 | tf_op jit(solution)/shard_map/psum | solution.py:61
  165.2 5.6 %copy-start.2 = (bf16[512,512]{1,0:T(8,128)(2,1)S(1)}, bf16[512,512]{1,0:T(8,128)(2,1)}, u32[]{:S(2)}) copy-start(bf16[512,512]{1,0:T(8,128)(2,1)} %param.10) | copy-start | bytes 1572868
  172.2 180.8 %copy-start.5 = (bf16[512,512]{1,0:T(8,128)(2,1)S(1)}, bf16[512,512]{1,0:T(8,128)(2,1)}, u32[]{:S(2)}) copy-start(bf16[512,512]{1,0:T(8,128)(2,1)} %param.11) | copy-start | bytes 1572868
Sparse Core Ops, SparseCore 0:
  124.6 219.1 reduce-scatter.1
Sparse Core Ops, SparseCore 1:
  170.9 267.5 all-reduce.2
